TPU v7x, 32 devices: a whole 2x2x4 slice. The times are simulated.
32 devices in a mesh: dom: 4 (over y, core), work: 8 (over z, x).
Axes of the slice: x: 2, y: 2, z: 4, core: 2. Of those that a mesh axis runs over, the one named last changes fastest.
Arguments:
- entity: float32 [4096, 400], P(('dom', 'work')), may hold values from -1.2 to 1.2
- row_state: float32 [4096], P(('dom', 'work')), may hold values from 0.001 to 0.03
- relation_table: bfloat16 [4096, 400], replicated, may hold values from -6 to 6
- edge_heads: int32 [16384], P(('dom', 'work')), may hold values from 0 to 1023, as said below
- edge_relations: int32 [16384], P(('dom', 'work')), may hold values from 0 to 4095
- edge_tails: int32 [16384], P(('dom', 'work')), may hold values from 0 to 1023, as said below
- plan: int32 [4], replicated, may hold values from 0 to 3, as said below
- negative_start: int32 [4], replicated, may hold values from 0 to 1023
Outputs:
- entity_new: float32 [4096, 400], P(('dom', 'work'))
- state_new: float32 [4096], P(('dom', 'work'))
Inputs may be any that keep to these rules, and one draw needn't show every extreme that they name: plan is a permutation of the groups. `edge_heads`: the edges held by worker w of a group have heads in rows w * 128 to (w + 1) * 128 - 1 of the group's partition. `edge_tails`: of the edges of one device at most 80 have tails in rows w * 128 to (w + 1) * 128 - 1 for any w, and on every device some w has exactly 80.
All inputs are finite; a program needn't handle non-finite values.
Results may differ from a plain program's by a relative error of at most 0.0003.
The roundings to bfloat16 on the way count: a program that leaves them out, or rounds other values in their place, can miss the bound.
Values may be sent and summed in bfloat16 or wider, within the bound.
A program may use at most 64 MiB of HBM per device.

v0:
```python
import math

import jax
import jax.numpy as jnp
from jax import lax
from jax.sharding import PartitionSpec as P

NEG = 1024


learn_rate = 0.1


def complex_query(head_rows, rel_rows):
    half_width = head_rows.shape[-1] // 2
    head_float = head_rows.astype(jnp.float32)
    relation = rel_rows.astype(jnp.float32)
    head_real, head_imaginary = (head_float[:, :half_width], head_float[:, half_width:])
    relation_real, relation_imaginary = (relation[:, :half_width], relation[:, half_width:])
    first = head_real * relation_real - head_imaginary * relation_imaginary
    second = head_real * relation_imaginary + head_imaginary * relation_real
    return jnp.concatenate([first, second], axis=1).astype(jnp.bfloat16)


def head_gradient(query_grad, rel_rows):
    half_width = query_grad.shape[-1] // 2
    relation = rel_rows.astype(jnp.float32)
    grad_real, grad_imaginary = (query_grad[:, :half_width], query_grad[:, half_width:])
    relation_real, relation_imaginary = (relation[:, :half_width], relation[:, half_width:])
    first = grad_real * relation_real + grad_imaginary * relation_imaginary
    second = grad_imaginary * relation_real - grad_real * relation_imaginary
    return jnp.concatenate([first, second], axis=1)


def negative_pass(queries, negatives, block_rows):
    edge_count, features = queries.shape
    num_blocks = edge_count // block_rows
    stacked = queries.reshape(num_blocks, block_rows, features)
    factor = 1.0 / math.sqrt(negatives.shape[0])

    def one_block(negative_grad, block_queries):
        scores = jnp.dot(block_queries, negatives.T, preferred_element_type=jnp.float32)
        weights = (jax.nn.sigmoid(scores) * factor).astype(jnp.bfloat16)
        pulled = jnp.dot(weights, negatives, preferred_element_type=jnp.float32)
        negative_grad = negative_grad + jnp.dot(
            weights.T, block_queries, preferred_element_type=jnp.float32
        )
        return (negative_grad, pulled)

    zero_grad = jnp.zeros((negatives.shape[0], features), jnp.float32)
    negative_grad, pulled = lax.scan(one_block, zero_grad, stacked)
    return (pulled.reshape(edge_count, features), negative_grad)


def block_rows_of(negative_grad, row_count, negative_first, part_rows):
    negative_count = negative_grad.shape[0]
    offsets = (jnp.arange(row_count, dtype=jnp.int32) - negative_first) % part_rows
    picked = jnp.take(negative_grad, jnp.minimum(offsets, negative_count - 1), axis=0)
    return jnp.where((offsets < negative_count)[:, None], picked, 0.0)


def body(
    entity, row_state, relation_table, edge_heads, edge_relations, edge_tails, plan, negative_start
):
    ent_rows, features = entity.shape
    edge_count = edge_heads.shape[0]
    workers = lax.axis_size("work")
    domains = lax.axis_size("dom")
    part_rows = ent_rows * workers
    domain_index = lax.axis_index("dom")
    worker = lax.axis_index("work")
    target = plan[domain_index]
    table = entity.astype(jnp.bfloat16)
    all_parts = lax.all_gather(table, "dom", axis=0, tiled=True)
    target_shard = lax.dynamic_slice_in_dim(all_parts, target * ent_rows, ent_rows, 0)
    target_part = lax.all_gather(target_shard, "work", axis=0, tiled=True)
    head_local = edge_heads - worker * ent_rows
    head_rows = jnp.take(table, head_local, axis=0)
    tail_rows = jnp.take(target_part, edge_tails, axis=0)
    rel_rows = jnp.take(relation_table, edge_relations, axis=0)
    queries = complex_query(head_rows, rel_rows)
    negative_first = negative_start[domain_index]
    negative_rows = (negative_first + jnp.arange(NEG, dtype=jnp.int32)) % part_rows
    negatives = jnp.take(target_part, negative_rows, axis=0)
    positive = jnp.sum(queries.astype(jnp.float32) * tail_rows.astype(jnp.float32), axis=1)
    positive_weight = jax.nn.sigmoid(positive) - 1.0
    pulled, negative_grad = negative_pass(queries, negatives, min(512, edge_count))
    query_grad = positive_weight[:, None] * tail_rows.astype(jnp.float32) + pulled
    own_grad = jax.ops.segment_sum(
        head_gradient(query_grad, rel_rows), head_local, num_segments=ent_rows
    )
    tail_grad = positive_weight[:, None] * queries.astype(jnp.float32)
    row_count = lax.axis_size("work") * ent_rows
    inside = (edge_tails >= 0) & (edge_tails < row_count)
    partial_value = jax.ops.segment_sum(
        tail_grad, jnp.where(inside, edge_tails, row_count), num_segments=row_count
    )
    target_grad = lax.psum_scatter(
        partial_value + block_rows_of(negative_grad, row_count, negative_first, part_rows),
        "work",
        scatter_dimension=0,
        tiled=True,
    )
    holder = jnp.zeros((domains * ent_rows, features), jnp.float32)
    holder = lax.dynamic_update_slice_in_dim(holder, target_grad, target * ent_rows, 0)
    returned = lax.psum_scatter(holder, "dom", scatter_dimension=0, tiled=True)
    gradient = own_grad + returned
    state_new = row_state + jnp.mean(gradient * gradient, axis=1)
    entity_new = entity - learn_rate * gradient / jnp.sqrt(state_new)[:, None]
    return (entity_new, state_new)


def solution(mesh):
    return jax.shard_map(
        body,
        mesh=mesh,
        in_specs=(
            P(("dom", "work"), None),
            P(("dom", "work")),
            P(),
            P(("dom", "work")),
            P(("dom", "work")),
            P(("dom", "work")),
            P(),
            P(),
        ),
        out_specs=(P(("dom", "work"), None), P(("dom", "work"))),
        check_vma=False,
    )
```

profile of v0, /device:TPU:1, one launch (start us, length us, event | category | flops | bytes accessed | tf_op | source)
XLA Modules:
  0.0 210.3 jit_solution(2002777509811293453)
XLA Ops:
  7.2 1.2 dynamic_slice.12
  13.2 1.2 dynamic_slice.13
  15.1 1.1 copy.25
  16.2 8.5 %all_gather.6 = bf16[512,400]{1,0:T(8,128)(2,1)S(1)} all-gather(bf16[128,400]{1,0:T(8,128)(2,1)S(1)} %convert_element_type.23), channel_id=1, replica_groups=mesh['dom'=4,'work'=8] {'dom'}, dimensions={0}, use_global_device_ids=true | all-gather | bytes 512000 | tf_op jit(solution)/shard_map/all_gather | solution.py:74
  24.8 27.7 %all_gather.7 = bf16[1024,400]{1,0:T(8,128)(2,1)S(1)} all-gather(bf16[128,400]{1,0:T(8,128)(2,1)S(1)} %constant_dynamic-slice_fusion), channel_id=1, replica_groups=mesh['dom'=4,'work'=8] {'work'}, dimensions={0}, use_global_device_ids=true | all-gather | bytes 921600 | tf_op jit(solution)/shard_map/all_gather | solution.py:76
  52.5 2.0 gather_fusion
  54.7 6.0 %copy.19 = bf16[4096,400]{1,0:T(8,128)(2,1)} copy(bf16[4096,400]{0,1:T(8,128)(2,1)} %param.10) | data formatting | bytes 6553600 | tf_op args[2]
  60.7 4.7 %gather_fusion.1 = bf16[512,400]{1,0:T(8,128)(2,1)S(1)} fusion(bf16[4096,400]{1,0:T(8,128)(2,1)} %copy.19, s32[1024]{0:T(1024)S(1)} %pad_clamp_fusion.1), kind=kCustom, calls=%fused_computation.1 | custom fusion | bytes 821248 | tf_op jit(solution)/shard_map/jit(_take)/gather | solution.py:80
  65.7 5.1 %gather_fusion.2 = bf16[1024,400]{1,0:T(8,128)(2,1)} fusion(bf16[1024,400]{1,0:T(8,128)(2,1)S(1)} %all_gather.7, s32[1024]{0:T(1024)S(1)} %broadcast_clamp_fusion.1), kind=kCustom, calls=%fused_computation.2 | custom fusion | bytes 1642496 | tf_op jit(solution)/shard_map/jit(_take)/gather | solution.py:84
  70.7 2.0 gather_fusion.4
  75.0 1.1 multiply_convert_fusion
  76.2 1.0 copy-done.5
  77.9 1.0 convert_multiply_fusion.2
  78.9 2.5 %copy.23 = f32[512,400]{1,0:T(8,128)} copy(f32[512,400]{0,1:T(8,128)} %convert_multiply_fusion.2) | data formatting | bytes 1638400 | tf_op jit(solution)/shard_map/mul | solution.py:92
  81.4 4.9 %gather_fusion.3 = f32[1024,400]{1,0:T(8,128)} fusion(f32[1024,400]{1,0:T(8,128)S(1)} %fusion.14, s32[1024]{0:T(1024)S(1)} %broadcast_clamp_fusion), kind=kCustom, calls=%fused_computation.3 | custom fusion | bytes 3280896 | tf_op jit(solution)/shard_map/jit(_take)/gather | solution.py:58
  86.3 2.2 %select_select_fusion = f32[1024,400]{1,0:T(8,128)S(1)} fusion(f32[1024,400]{1,0:T(8,128)} %gather_fusion.3, pred[1024]{0:T(1024)(128)(4,1)S(1)} %get-tuple-element.31, pred[1024]{0:T(1024)(128)(4,1)S(1)} %get-tuple-element.32), kind=kLoop, calls=%fused_computation.7 | loop fusion | flops 819200 | bytes 3278848 | tf_op jit(solution)/shard_map/jit(_where)/select_n | solution.py:59
  88.4 5.0 %scatter_fusion = f32[1024,400]{1,0:T(8,128)S(1)} fusion(f32[1024,400]{1,0:T(8,128)S(1)} %select_select_fusion, s32[512]{0:T(512)S(1)} %get-tuple-element.28, f32[512,400]{1,0:T(8,128)} %copy.23), kind=kCustom, calls=%fused_computation.5 | custom fusion | flops 204800 | bytes 2459648 | tf_op jit(solution)/shard_map/scatter-add | solution.py:95
  93.5 1.3 copy-done
  95.1 71.4 %reduce-scatter.3.cloned.1.call-done = f32[128,400]{1,0:T(8,128)} async-done(((f32[1024,400]{1,0:T(8,128)}), f32[128,400]{1,0:T(8,128)}) %reduce-scatter.3.cloned.1.call-update) | async-done | bytes 204816 | tf_op jit(solution)/shard_map/reduce_scatter | solution.py:98
  168.6 2.3 %convolution_add_fusion = f32[512,400]{0,1:T(8,128)S(1)} fusion(bf16[512,1024]{1,0:T(8,128)(2,1)} %copy-done.5, bf16[1024,400]{1,0:T(8,128)(2,1)} %gather_fusion.2, pred[1024]{0:T(1024)(128)(4,1)S(1)} %compare_and_fusion, f32[512]{0:T(512)S(1)} %divide_add_fusion, bf16[512,400]{0,1:T(8,128)(2,1)S(1)} %copy-done.3, pred[512]{0:T(512)(128)(4,1)S(1)} %compare_and_fusion.2), kind=kOutput, calls=%fused_computation.9 | convolution fusion | flops 420659200 | bytes 3100160 | tf_op jit(solution)/shard_map/while/body/eval_jaxpr/dot_general | solution.py:44
  171.5 23.3 %reduce-scatter.5.cloned.1.call-done = f32[128,400]{1,0:T(8,128)} async-done(((f32[512,400]{1,0:T(8,128)}), f32[128,400]{1,0:T(8,128)}) %reduce-scatter.5.cloned.1.call-update) | async-done | bytes 204816 | tf_op jit(solution)/shard_map/reduce_scatter | solution.py:106
  194.8 5.2 %scatter_fusion.1 = f32[128,400]{1,0:T(8,128)} fusion(f32[128,400]{1,0:T(8,128)} %reduce-scatter.5.cloned.1.call-done, s32[512]{0:T(512)S(1)} %get-tuple-element.22, f32[512,400]{1,0:T(8,128)S(1)} %copy.24), kind=kCustom, calls=%fused_computation.6 | custom fusion | flops 204800 | bytes 2459648 | tf_op jit(solution)/shard_map/scatter-add | solution.py:89
  200.0 1.1 multiply_reduce_fusion
  201.6 1.0 divide_subtract_fusion
  (50 shorter events, 12.5 us)
Async XLA Ops:
  7.2 45.3 %copy-start.6 = (s32[512]{0:T(512)S(1)}, s32[512]{0:T(512)}, u32[]{:S(2)}) copy-start(s32[512]{0:T(512)} %param.11) | copy-start | bytes 6148
  7.2 159.3 %reduce-scatter.3.cloned.1.call-start = ((), (), s32[]{:S(2)}) async-start(), calls=%async_computation.2 | async-start | bytes 2359296 | tf_op jit(solution)/shard_map/reduce_scatter | solution.py:98
  73.6 1.0 copy-start.2
  73.7 1.3 copy-start.4
  76.2 1.0 copy-start.5
  93.5 1.3 copy-start
  94.8 73.8 %copy-start.3 = (bf16[512,400]{0,1:T(8,128)(2,1)S(1)}, bf16[512,400]{0,1:T(8,128)(2,1)}, u32[]{:S(2)}) copy-start(bf16[512,400]{0,1:T(8,128)(2,1)} %copy.22) | copy-start | bytes 1228804
  94.8 100.0 %reduce-scatter.5.cloned.1.call-start = ((), (), s32[]{:S(2)}) async-start(), calls=%async_computation.3 | async-start | bytes 1310720 | tf_op jit(solution)/shard_map/reduce_scatter | solution.py:106
  167.6 1.0 copy-start.1
  171.5 29.6 %copy-start.7 = (f32[128]{0:T(128)S(1)}, f32[128]{0:T(128)}, u32[]{:S(2)}) copy-start(f32[128]{0:T(128)} %param.9) | copy-start | bytes 1540
Sparse Core Ops, SparseCore 0:
  95.0 71.5 reduce-scatter.2
  169.0 25.7 reduce-scatter.4
where the time goes:
time: 212 us; the launch traced here: 210 us
  waiting for transfers between devices  94.8 us (45%)
  local copies, waits for them, and re-layouts  38.3 us (18%)
  blocking collectives  36.2 us (17%)
  other arithmetic  21.6 us (10%)
  between operations  15 us (7%)
  matrix products  4.23 us (2%)
    reduce_scatter x1, waiting for transfers between devices, body(): lax.psum_scatter(partial_value + block_rows_of(negative_grad, row_count,...  71.4 us
    all_gather x1, blocking collectives, body(): target_part = lax.all_gather(target_shard, 'work', axis=0, tiled=True)  27.7 us
    reduce_scatter x1, waiting for transfers between devices, body(): returned = lax.psum_scatter(holder, 'dom', scatter_dimension=0, tiled=True)  23.3 us
    unnamed x19, local copies, waits for them, and re-layouts  12 us
    all_gather x1, blocking collectives, body(): all_parts = lax.all_gather(table, 'dom', axis=0, tiled=True)  8.54 us
    scatter-add x1, other arithmetic, body(): jax.ops.segment_sum(head_gradient(query_grad, rel_rows), head_local, num_...  5.17 us
    gather x1, local copies, waits for them, and re-layouts, body(): negatives = jnp.take(target_part, negative_rows, axis=0)  5.06 us
    scatter-add x1, other arithmetic, body(): jax.ops.segment_sum(tail_grad, jnp.where(inside, edge_tails, row_count),...  5.03 us
  transfers between devices with their start and end apart: 2, of which 2 were waited for; matrix products, arithmetic and copies ran while one was open for 1% of the time, Pallas kernels for 0%

commit v1 on v0

v1 whole, which is shorter than its diff:
```python
import functools
import math

import jax
import jax.numpy as jnp
from jax import lax
from jax.experimental import pallas as pl
from jax.experimental.pallas import tpu as pltpu
from jax.sharding import PartitionSpec as P

NEG = 1024
learn_rate = 0.1
MESH = pl.DeviceIdType.MESH
F32 = jnp.float32
BF16 = jnp.bfloat16
GRAD = F32


def dot_nn(a, b):
    return lax.dot_general(a, b, (((1,), (0,)), ((), ())), preferred_element_type=F32)


def dot_nt(a, b):
    return lax.dot_general(a, b, (((1,), (1,)), ((), ())), preferred_element_type=F32)


def split(value):
    high = value.astype(BF16)
    low = (value - high.astype(F32)).astype(BF16)
    return high, low


def transpose_pad(value):
    n, m = value.shape
    pad = -m % 128
    if pad:
        value = jnp.concatenate([value, jnp.zeros((n, pad), value.dtype)], axis=1)
    return jnp.transpose(value)[:m]


def untranspose_pad(value):
    m, n = value.shape
    pad = -m % 128
    if pad:
        value = jnp.concatenate([value, jnp.zeros((pad, n), value.dtype)], axis=0)
    return jnp.transpose(value)[:, :m]


def kernel(
    domains,
    workers,
    entity_ref,
    state_ref,
    relation_hbm,
    heads_ref,
    relations_ref,
    tails_ref,
    plan_ref,
    start_ref,
    entity_out,
    state_out,
    relation_vmem,
    parts,
    target_part,
    partial,
    summed,
    returned,
    rel_rows,
    pulled,
    query_t,
    query_e,
    tail_hi,
    tail_lo,
    relation_sem,
    parts_send,
    parts_recv,
    target_send,
    target_recv,
    sum_send,
    sum_recv,
    return_send,
    return_recv,
):
    rows, features = entity_ref.shape
    half = features // 2
    edges = heads_ref.shape[1]
    relations = relation_hbm.shape[0]
    part_rows = rows * workers
    dom = lax.axis_index("dom")
    me = lax.axis_index("work")

    relation_copy = pltpu.make_async_copy(relation_hbm, relation_vmem, relation_sem)
    relation_copy.start()

    barrier = pltpu.get_barrier_semaphore()

    def dom_peer(k):
        return lax.rem(dom + k, domains)

    def work_peer(k):
        return lax.rem(me + k, workers)

    def from_dom(k):
        return lax.rem(dom + domains - k, domains)

    def from_work(k):
        return lax.rem(me + workers - k, workers)

    for k in range(1, domains):
        pl.semaphore_signal(barrier, inc=1, device_id=(dom_peer(k), me), device_id_type=MESH)
    for k in range(1, workers):
        pl.semaphore_signal(barrier, inc=1, device_id=(dom, work_peer(k)), device_id_type=MESH)

    entity_t = transpose_pad(entity_ref[...])
    table_t = entity_t.astype(BF16)
    parts[dom] = table_t
    pl.semaphore_wait(barrier, domains + workers - 2)

    def parts_copy(k):
        return pltpu.make_async_remote_copy(
            src_ref=parts.at[dom],
            dst_ref=parts.at[dom],
            send_sem=parts_send.at[k],
            recv_sem=parts_recv.at[k],
            device_id=(dom_peer(k), me),
            device_id_type=MESH,
        )

    def parts_arrival(k):
        return pltpu.make_async_remote_copy(
            src_ref=parts.at[from_dom(k)],
            dst_ref=parts.at[from_dom(k)],
            send_sem=parts_send.at[k],
            recv_sem=parts_recv.at[k],
            device_id=(dom_peer(k), me),
            device_id_type=MESH,
        )

    for k in range(1, domains):
        parts_copy(k).start()

    head_local = heads_ref[...] - me * rows
    head_hot = (
        lax.broadcasted_iota(jnp.int32, (rows, edges), 0) == head_local
    ).astype(F32).astype(BF16)
    head_t = dot_nn(table_t, head_hot)

    for k in range(1, domains):
        parts_arrival(k).wait_recv()
    target = plan_ref[dom]
    target_part[me] = parts[target]

    def target_copy(k):
        return pltpu.make_async_remote_copy(
            src_ref=target_part.at[me],
            dst_ref=target_part.at[me],
            send_sem=target_send.at[k],
            recv_sem=target_recv.at[k],
            device_id=(dom, work_peer(k)),
            device_id_type=MESH,
        )

    def target_arrival(k):
        return pltpu.make_async_remote_copy(
            src_ref=target_part.at[from_work(k)],
            dst_ref=target_part.at[from_work(k)],
            send_sem=target_send.at[k],
            recv_sem=target_recv.at[k],
            device_id=(dom, work_peer(k)),
            device_id_type=MESH,
        )

    for k in range(1, workers):
        target_copy(k).start()

    relation_index = jnp.transpose(
        jnp.broadcast_to(relations_ref[...], (128, edges)).astype(F32)
    ).astype(jnp.int32)
    relation_copy.wait()
    rel_rows[...] = jnp.zeros_like(rel_rows)
    step_rows = 512

    def relation_step(step, carry):
        base = pl.multiple_of(step * step_rows, step_rows)
        lane = lax.broadcasted_iota(jnp.int32, (edges, 128), 1)
        hot = jnp.concatenate(
            [
                (relation_index == lane + (base + j * 128)).astype(F32).astype(BF16)
                for j in range(step_rows // 128)
            ],
            axis=1,
        )
        rel_rows[...] += dot_nn(hot, relation_vmem[pl.ds(base, step_rows), :])
        return carry

    lax.fori_loop(0, relations // step_rows, relation_step, 0)
    rel_t = transpose_pad(rel_rows[...])
    rel_x, rel_y = rel_t[:half], rel_t[half:]
    head_x, head_y = head_t[:half], head_t[half:]
    query = jnp.concatenate(
        [head_x * rel_x - head_y * rel_y, head_x * rel_y + head_y * rel_x], axis=0
    )
    query_bf = query.astype(BF16)
    query_t[...] = query_bf
    query_float = query_bf.astype(F32)
    query_e[...] = untranspose_pad(query_float).astype(BF16)

    for k in range(1, workers):
        target_arrival(k).wait_recv()

    def tail_hot(first, count):
        row = lax.broadcasted_iota(jnp.int32, (count, edges), 0) + first
        return (row == tails_ref[...]).astype(F32).astype(BF16)

    pair = 2
    width = pair * rows

    def pair_of(block):
        return jnp.concatenate([target_part[block * pair + j] for j in range(pair)], axis=1)

    pulled[...] = jnp.zeros_like(pulled)

    def tail_step(block, carry):
        pulled[...] += dot_nn(pair_of(block), tail_hot(block * width, width))
        return carry

    lax.fori_loop(0, workers // pair, tail_step, 0)
    tail_t = pulled[...]
    positive = jnp.sum(query_float * tail_t, axis=0, keepdims=True)
    positive_weight = jax.nn.sigmoid(positive) - 1.0
    pulled[...] = positive_weight * tail_t
    high, low = split(positive_weight * query_float)
    tail_hi[...] = high
    tail_lo[...] = low
    factor = 1.0 / math.sqrt(NEG)
    first_negative = start_ref[dom]

    def sum_copy(dest, k):
        return pltpu.make_async_remote_copy(
            src_ref=partial.at[dest],
            dst_ref=summed.at[me],
            send_sem=sum_send.at[dest],
            recv_sem=sum_recv.at[me],
            device_id=(dom, dest),
            device_id_type=MESH,
        )

    def sum_arrival(source):
        return pltpu.make_async_remote_copy(
            src_ref=partial.at[source],
            dst_ref=summed.at[source],
            send_sem=sum_send.at[source],
            recv_sem=sum_recv.at[source],
            device_id=(dom, source),
            device_id_type=MESH,
        )

    def score_step(step, carry):
        block = lax.rem(me // pair + step + 1, workers // pair)
        part = pair_of(block)
        scores = dot_nn(query_e[...], part)
        row = lax.broadcasted_iota(jnp.int32, (1, width), 1) + block * width
        offset = row - first_negative
        offset = jnp.where(offset < 0, offset + part_rows, offset)
        weights = jax.nn.sigmoid(scores) * factor
        if part_rows > NEG:
            weights = jnp.where(offset < NEG, weights, 0.0)
        weights = weights.astype(BF16)
        pulled[...] += dot_nt(part, weights)
        hot = tail_hot(block * width, width)
        grad = (
            dot_nn(query_t[...], weights) + dot_nt(tail_hi[...], hot) + dot_nt(tail_lo[...], hot)
        )
        for j in range(pair):
            dest = block * pair + j
            partial[dest] = grad[:, j * rows : (j + 1) * rows].astype(GRAD)

            @pl.when(dest != me)
            def _():
                sum_copy(dest, 0).start()

        return carry

    lax.fori_loop(0, workers // pair, score_step, 0)

    grad_t = pulled[...]
    grad_x, grad_y = grad_t[:half], grad_t[half:]
    rel_t = transpose_pad(rel_rows[...])
    rel_x, rel_y = rel_t[:half], rel_t[half:]
    head_grad = jnp.concatenate(
        [grad_x * rel_x + grad_y * rel_y, grad_y * rel_x - grad_x * rel_y], axis=0
    )
    high, low = split(head_grad)
    own_grad = dot_nt(high, head_hot) + dot_nt(low, head_hot)

    total = partial[me].astype(F32)
    for k in range(1, workers):
        source = from_work(k)
        sum_arrival(source).wait_recv()
        total = total + summed[source].astype(F32)
    returned[dom] = total.astype(GRAD)

    def return_copy(k):
        return pltpu.make_async_remote_copy(
            src_ref=returned.at[dom],
            dst_ref=returned.at[dom],
            send_sem=return_send.at[k],
            recv_sem=return_recv.at[k],
            device_id=(dom_peer(k), me),
            device_id_type=MESH,
        )

    def return_arrival(k):
        return pltpu.make_async_remote_copy(
            src_ref=returned.at[from_dom(k)],
            dst_ref=returned.at[from_dom(k)],
            send_sem=return_send.at[k],
            recv_sem=return_recv.at[k],
            device_id=(dom_peer(k), me),
            device_id_type=MESH,
        )

    for k in range(1, domains):
        return_copy(k).start()
    giver = jnp.int32(0)
    for p in range(1, domains):
        giver = jnp.where(plan_ref[p] == dom, jnp.int32(p), giver)
    for k in range(1, domains):
        return_arrival(k).wait_recv()
    gradient = own_grad + returned[giver].astype(F32)
    state_new = state_ref[...] + jnp.sum(gradient * gradient, axis=0, keepdims=True) / features
    state_out[...] = state_new
    entity_new = transpose_pad(entity_ref[...]) - learn_rate * gradient / jnp.sqrt(state_new)
    entity_out[...] = untranspose_pad(entity_new)

    for k in range(1, domains):
        parts_copy(k).wait_send()
        return_copy(k).wait_send()
    for k in range(1, workers):
        target_copy(k).wait_send()
        sum_copy(work_peer(k), k).wait_send()


def body(
    domains,
    workers,
    entity,
    row_state,
    relation_table,
    edge_heads,
    edge_relations,
    edge_tails,
    plan,
    negative_start,
):
    rows, features = entity.shape
    edges = edge_heads.shape[0]
    vmem = pl.BlockSpec(memory_space=pltpu.VMEM)
    smem = pl.BlockSpec(memory_space=pltpu.SMEM)
    entity_new, state_new = pl.pallas_call(
        functools.partial(kernel, domains, workers),
        out_shape=(
            jax.ShapeDtypeStruct((rows, features), F32),
            jax.ShapeDtypeStruct((1, rows), F32),
        ),
        in_specs=[vmem, vmem, pl.BlockSpec(memory_space=pl.ANY), vmem, vmem, vmem, smem, smem],
        out_specs=(vmem, vmem),
        scratch_shapes=[
            pltpu.VMEM(relation_table.shape, BF16),
            pltpu.VMEM((domains, features, rows), BF16),
            pltpu.VMEM((workers, features, rows), BF16),
            pltpu.VMEM((workers, features, rows), GRAD),
            pltpu.VMEM((workers, features, rows), GRAD),
            pltpu.VMEM((domains, features, rows), GRAD),
            pltpu.VMEM((edges, features), F32),
            pltpu.VMEM((features, edges), F32),
            pltpu.VMEM((features, edges), BF16),
            pltpu.VMEM((edges, features), BF16),
            pltpu.VMEM((features, edges), BF16),
            pltpu.VMEM((features, edges), BF16),
            pltpu.SemaphoreType.DMA,
            pltpu.SemaphoreType.DMA((domains,)),
            pltpu.SemaphoreType.DMA((domains,)),
            pltpu.SemaphoreType.DMA((workers,)),
            pltpu.SemaphoreType.DMA((workers,)),
            pltpu.SemaphoreType.DMA((workers,)),
            pltpu.SemaphoreType.DMA((workers,)),
            pltpu.SemaphoreType.DMA((domains,)),
            pltpu.SemaphoreType.DMA((domains,)),
        ],
        compiler_params=pltpu.CompilerParams(
            collective_id=0, has_side_effects=True, vmem_limit_bytes=50 << 20
        ),
    )(
        entity,
        row_state.reshape(1, rows),
        relation_table,
        edge_heads.reshape(1, edges),
        edge_relations.reshape(1, edges),
        edge_tails.reshape(1, edges),
        plan,
        negative_start,
    )
    return entity_new, state_new.reshape(rows)


def solution(mesh):
    return jax.shard_map(
        functools.partial(body, mesh.shape["dom"], mesh.shape["work"]),
        mesh=mesh,
        in_specs=(
            P(("dom", "work"), None),
            P(("dom", "work")),
            P(),
            P(("dom", "work")),
            P(("dom", "work")),
            P(("dom", "work")),
            P(),
            P(),
        ),
        out_specs=(P(("dom", "work"), None), P(("dom", "work"))),
        check_vma=False,
    )
```

time: 212 us -> 88.5 us (0.42)
  the two profiles are of different devices: /device:TPU:1 before, /device:TPU:27 now
where the time goes in v1:
time: 88.5 us; the launch traced here: 88.3 us
  Pallas kernels  79.1 us (89%)
  local copies, waits for them, and re-layouts  8.44 us (10%)
    pallas_call x1, Pallas kernels, body(): pl.pallas_call(functools.partial(kernel, domains, workers), out_shape=(ja...  79.1 us
    unnamed x16, local copies, waits for them, and re-layouts  8.44 us

profile of v1, /device:TPU:27, one launch (start us, length us, event | category | flops | bytes accessed | tf_op | source)
XLA Modules:
  0.0 88.3 jit_solution(10901583787894889595)
XLA Ops:
  0.6 0.0 copy-start.5
  0.6 0.0 copy-start.4
  0.7 0.0 copy-start.2
  0.7 0.0 copy-start.1
  0.7 0.0 copy-start
  0.7 0.0 copy-start.3
  0.7 1.1 %copy.10.entity_ref = f32[128,400]{1,0:T(8,128)S(1)} copy(f32[128,400]{0,1:T(8,128)} %param.8) | data formatting | bytes 409600 | tf_op args[0]
  1.8 6.0 %copy.11.relation_hbm = bf16[4096,400]{1,0:T(8,128)(2,1)} copy(bf16[4096,400]{0,1:T(8,128)(2,1)} %param.10) | data formatting | bytes 6553600 | tf_op args[2]
  7.8 0.0 copy-done.5
  7.8 0.0 copy-done.4
  7.8 0.0 copy-done.2
  7.8 0.0 copy-done.1
  7.8 0.0 copy-done
  7.8 0.0 copy-done.3
  7.8 79.1 %shard_map.95 = (f32[128,400]{1,0:T(8,128)S(1)}, f32[1,128]{1,0:T(1,128)S(1)}) custom-call(f32[128,400]{1,0:T(8,128)S(1)} %copy.10.entity_ref, f32[1,128]{1,0:T(1,128)S(1)} %bitcast.8, bf16[4096,400]{1,0:T(8,128)(2,1)} %copy.11.relation_hbm, s32[1,512]{1,0:T(1,128)S(1)} %bitcast.5, s32[1,512]{1,0:T(1,128)S(1)} %bitcast.6, s32[1,512]{1,0:T(1,128)S(1)} %bitcast.7, ...), custom_call_target="tpu_custom_call" | custom-call | tf_op jit(solution)/shard_map/pallas_call | solution.py:360
  86.9 0.8 copy.12
  87.8 0.5 copy.14
Async XLA Ops:
  0.6 7.2 %copy-start.5 = (s32[4]{0:T(128)S(1)}, s32[4]{0:T(128)}, u32[]{:S(2)}) copy-start(s32[4]{0:T(128)} %start_ref.1) | copy-start | bytes 52
  0.6 7.2 %copy-start.4 = (s32[4]{0:T(128)S(1)}, s32[4]{0:T(128)}, u32[]{:S(2)}) copy-start(s32[4]{0:T(128)} %plan_ref.1) | copy-start | bytes 52
  0.7 7.1 %copy-start.2 = (s32[512]{0:T(512)S(1)}, s32[512]{0:T(512)}, u32[]{:S(2)}) copy-start(s32[512]{0:T(512)} %param.13) | copy-start | bytes 6148
  0.7 7.1 %copy-start.1 = (s32[512]{0:T(512)S(1)}, s32[512]{0:T(512)}, u32[]{:S(2)}) copy-start(s32[512]{0:T(512)} %param.12) | copy-start | bytes 6148
  0.7 7.1 %copy-start = (s32[512]{0:T(512)S(1)}, s32[512]{0:T(512)}, u32[]{:S(2)}) copy-start(s32[512]{0:T(512)} %param.11) | copy-start | bytes 6148
  0.7 7.1 %copy-start.3 = (f32[128]{0:T(128)S(1)}, f32[128]{0:T(128)}, u32[]{:S(2)}) copy-start(f32[128]{0:T(128)} %param.9) | copy-start | bytes 1540

commit v2 on v1

v2 whole, which is shorter than its diff:
```python
import functools
import math

import jax
import jax.numpy as jnp
from jax import lax
from jax.experimental import pallas as pl
from jax.experimental.pallas import tpu as pltpu
from jax.sharding import PartitionSpec as P

NEG = 1024
learn_rate = 0.1
MESH = pl.DeviceIdType.MESH
F32 = jnp.float32
BF16 = jnp.bfloat16
CODE = jnp.int16


def dot_nn(a, b):
    return lax.dot_general(a, b, (((1,), (0,)), ((), ())), preferred_element_type=F32)


def dot_nt(a, b):
    return lax.dot_general(a, b, (((1,), (1,)), ((), ())), preferred_element_type=F32)


def split(value):
    high = value.astype(BF16)
    low = (value - high.astype(F32)).astype(BF16)
    return high, low


def untranspose_pad(value):
    m, n = value.shape
    pad = -m % 128
    if pad:
        value = jnp.concatenate([value, jnp.zeros((pad, n), value.dtype)], axis=0)
    return jnp.transpose(value)[:, :m]


def encode(value):
    largest = jnp.max(jnp.abs(value), axis=0, keepdims=True)
    exponent = jnp.ceil(jnp.log2(jnp.maximum(largest, 1e-30)) + 0.03)
    exponent = jnp.broadcast_to(exponent, (16, value.shape[1]))
    scale = jnp.exp2(15.0 - exponent)[:1]
    code = jnp.floor(value * scale + 0.5).astype(jnp.int32)
    return code.astype(CODE), exponent.astype(jnp.int32).astype(CODE)


def store_code(ref, slot, value):
    rows = value.shape[0]
    code, exponent = encode(value)
    ref[slot, :rows, :] = code
    ref[slot, rows:, :] = exponent


def load_code(ref, slot):
    whole = ref[slot].astype(jnp.int32).astype(F32)
    rows = whole.shape[0] - 16
    scale = jnp.exp2(whole[rows:] - 15.0)[:1]
    return whole[:rows] * scale


class Exchange:
    def __init__(self, ref, device, a, b, a_size, b_size, sems):
        self.ref, self.device = ref, device
        self.a, self.b, self.a_size, self.b_size = a, b, a_size, b_size
        self.a_send, self.a_recv, self.b_send, self.b_recv = sems

    def slot(self, ka, kb):
        a = lax.rem(self.a + self.a_size - ka, self.a_size)
        b = lax.rem(self.b + self.b_size - kb, self.b_size)
        return a * self.b_size + b

    def peer(self, ka, kb):
        a = lax.rem(self.a + ka, self.a_size)
        b = lax.rem(self.b + kb, self.b_size)
        return self.device(a * self.b_size + b)

    def copy(self, slot, peer, send, recv):
        return pltpu.make_async_remote_copy(
            src_ref=self.ref.at[slot],
            dst_ref=self.ref.at[slot],
            send_sem=send,
            recv_sem=recv,
            device_id=peer,
            device_id_type=MESH,
        )

    def first(self, k, arriving=False):
        slot = self.slot(k, 0) if arriving else self.slot(0, 0)
        return self.copy(slot, self.peer(k, 0), self.a_send.at[k], self.a_recv.at[k])

    def second(self, ka, kb, arriving=False):
        slot = self.slot(ka, kb) if arriving else self.slot(ka, 0)
        at = ka * self.b_size + kb
        return self.copy(slot, self.peer(0, kb), self.b_send.at[at], self.b_recv.at[at])

    def start(self):
        for k in range(1, self.a_size):
            self.first(k).start()
        for kb in range(1, self.b_size):
            self.second(0, kb).start()

    def forward(self, k):
        self.first(k, True).wait_recv()
        for kb in range(1, self.b_size):
            self.second(k, kb).start()

    def collect(self):
        for ka in range(self.a_size):
            for kb in range(1, self.b_size):
                self.second(ka, kb, True).wait_recv()

    def finish(self):
        for k in range(1, self.a_size):
            self.first(k).wait_send()
        for ka in range(self.a_size):
            for kb in range(1, self.b_size):
                self.second(ka, kb).wait_send()


def kernel(
    dom_shape,
    work_shape,
    entity_ref,
    state_ref,
    relation_hbm,
    heads_ref,
    relations_ref,
    tails_ref,
    plan_ref,
    start_ref,
    entity_out,
    state_out,
    relation_vmem,
    parts,
    target_part,
    partial,
    own_partial,
    across,
    along_out,
    along_in,
    returned,
    rel_t,
    pulled,
    query_t,
    query_e,
    tail_hi,
    tail_lo,
    relation_sem,
    *sems,
):
    features, rows = entity_ref.shape
    half = features // 2
    edges = heads_ref.shape[1]
    relations = relation_hbm.shape[1]
    chips, cores = dom_shape
    z_size, x_size = work_shape
    part_rows = rows * z_size * x_size
    dom = lax.axis_index("dom")
    me = lax.axis_index("work")
    y, core = dom // cores, lax.rem(dom, cores)
    z, x = me // x_size, lax.rem(me, x_size)

    relation_copy = pltpu.make_async_copy(relation_hbm, relation_vmem, relation_sem)
    relation_copy.start()

    def dom_device(index):
        return (index, me)

    def work_device(index):
        return (dom, index)

    part_exchange = Exchange(parts, dom_device, y, core, chips, cores, sems[0:4])
    target_exchange = Exchange(target_part, work_device, z, x, z_size, x_size, sems[4:8])
    return_exchange = Exchange(returned, dom_device, y, core, chips, cores, sems[8:12])
    across_send, across_recv, along_send, along_recv = sems[12:16]

    barrier = pltpu.get_barrier_semaphore()
    for exchange in (part_exchange, target_exchange):
        for k in range(1, exchange.a_size):
            pl.semaphore_signal(
                barrier, inc=1, device_id=exchange.peer(k, 0), device_id_type=MESH
            )
        for k in range(1, exchange.b_size):
            pl.semaphore_signal(
                barrier, inc=1, device_id=exchange.peer(0, k), device_id_type=MESH
            )

    table_t = entity_ref[...].astype(BF16)
    parts[dom] = table_t
    pl.semaphore_wait(barrier, chips + cores + z_size + x_size - 4)
    part_exchange.start()

    head_local = heads_ref[...] - me * rows
    head_hot = (
        lax.broadcasted_iota(jnp.int32, (rows, edges), 0) == head_local
    ).astype(F32).astype(BF16)
    head_t = dot_nn(table_t, head_hot)

    for k in range(1, chips):
        part_exchange.forward(k)
    part_exchange.collect()
    target_part[me] = parts[plan_ref[dom]]
    target_exchange.start()

    relation_copy.wait()
    rel_t[...] = jnp.zeros_like(rel_t)
    step_rows = 256

    def relation_step(step, carry):
        base = pl.multiple_of(step * step_rows, step_rows)
        row = lax.broadcasted_iota(jnp.int32, (step_rows, edges), 0) + base
        hot = (row == relations_ref[...]).astype(F32).astype(BF16)
        rel_t[...] += dot_nn(relation_vmem[:, pl.ds(base, step_rows)], hot)
        return carry

    steps = relations // step_rows
    for k in range(1, z_size + 1):
        lax.fori_loop((k - 1) * steps // z_size, k * steps // z_size, relation_step, 0)
        if k < z_size:
            target_exchange.forward(k)

    rel_x, rel_y = rel_t[:half], rel_t[half:]
    head_x, head_y = head_t[:half], head_t[half:]
    query = jnp.concatenate(
        [head_x * rel_x - head_y * rel_y, head_x * rel_y + head_y * rel_x], axis=0
    )
    query_bf = query.astype(BF16)
    query_t[...] = query_bf
    query_float = query_bf.astype(F32)
    query_e[...] = untranspose_pad(query_float).astype(BF16)

    target_exchange.collect()

    width = x_size * rows

    def tail_hot(block):
        row = lax.broadcasted_iota(jnp.int32, (width, edges), 0) + block * width
        return (row == tails_ref[...]).astype(F32).astype(BF16)

    def block_of(block):
        return jnp.concatenate([target_part[block * x_size + j] for j in range(x_size)], axis=1)

    pulled[...] = jnp.zeros_like(pulled)

    def tail_step(block, carry):
        pulled[...] += dot_nn(block_of(block), tail_hot(block))
        return carry

    lax.fori_loop(0, z_size, tail_step, 0)
    tail_t = pulled[...]
    positive = jnp.sum(query_float * tail_t, axis=0, keepdims=True)
    positive_weight = jax.nn.sigmoid(positive) - 1.0
    pulled[...] = positive_weight * tail_t
    high, low = split(positive_weight * query_float)
    tail_hi[...] = high
    tail_lo[...] = low
    factor = 1.0 / math.sqrt(NEG)
    first_negative = start_ref[dom]

    def across_copy(block, j, arriving=False):
        k = lax.rem(j - x + x_size, x_size)
        landing = (lax.rem(x_size - k, x_size) if arriving else k) * z_size + block
        return pltpu.make_async_remote_copy(
            src_ref=partial.at[block * x_size + j],
            dst_ref=across.at[landing],
            send_sem=across_send.at[block * x_size + j],
            recv_sem=across_recv.at[landing],
            device_id=(dom, z * x_size + j),
            device_id_type=MESH,
        )

    def along_copy(k):
        return pltpu.make_async_remote_copy(
            src_ref=along_out.at[k],
            dst_ref=along_in.at[k],
            send_sem=along_send.at[k],
            recv_sem=along_recv.at[k],
            device_id=(dom, lax.rem(z + k, z_size) * x_size + x),
            device_id_type=MESH,
        )

    def score_step(step, carry):
        block = lax.rem(z + step + 1, z_size)
        part = block_of(block)
        scores = dot_nn(query_e[...], part)
        weights = jax.nn.sigmoid(scores) * factor
        if part_rows > NEG:
            row = lax.broadcasted_iota(jnp.int32, (1, width), 1) + block * width
            offset = row - first_negative
            offset = jnp.where(offset < 0, offset + part_rows, offset)
            weights = jnp.where(offset < NEG, weights, 0.0)
        weights = weights.astype(BF16)
        hot = tail_hot(block)
        grad = (
            dot_nn(query_t[...], weights) + dot_nt(tail_hi[...], hot) + dot_nt(tail_lo[...], hot)
        )
        for j in range(x_size):
            piece = grad[:, j * rows : (j + 1) * rows]

            @pl.when(x == j)
            def _():
                own_partial[block] = piece

            @pl.when(x != j)
            def _():
                store_code(partial, block * x_size + j, piece)
                across_copy(block, j).start()

        pulled[...] += dot_nt(part, weights)
        return carry

    lax.fori_loop(0, z_size, score_step, 0)

    def own_gradient():
        grad_x, grad_y = pulled[:half], pulled[half:]
        rel_x, rel_y = rel_t[:half], rel_t[half:]
        head_grad = jnp.concatenate(
            [grad_x * rel_x + grad_y * rel_y, grad_y * rel_x - grad_x * rel_y], axis=0
        )
        high, low = split(head_grad)
        return dot_nt(high, head_hot) + dot_nt(low, head_hot)

    own_grad = None
    for step in range(1, z_size + 1):
        block = lax.rem(z + step, z_size)
        total = own_partial[block]
        for k in range(1, x_size):
            across_copy(block, lax.rem(x + x_size - k, x_size), True).wait_recv()
            total = total + load_code(across, k * z_size + block)
        if step < z_size:
            store_code(along_out, step, total)
            along_copy(step).start()
        if step == 1:
            own_grad = own_gradient()
    for k in range(1, z_size):
        along_copy(k).wait_recv()
        total = total + load_code(along_in, k)
    store_code(returned, dom, total)
    return_exchange.start()
    giver = jnp.int32(0)
    for p in range(1, chips * cores):
        giver = jnp.where(plan_ref[p] == dom, jnp.int32(p), giver)
    for k in range(1, chips):
        return_exchange.forward(k)
    return_exchange.collect()
    gradient = own_grad + load_code(returned, giver)
    state_new = state_ref[...] + jnp.sum(gradient * gradient, axis=0, keepdims=True) / features
    state_out[...] = state_new
    entity_out[...] = entity_ref[...] - learn_rate * gradient / jnp.sqrt(state_new)

    part_exchange.finish()
    target_exchange.finish()
    return_exchange.finish()
    for k in range(1, z_size):
        along_copy(k).wait_send()
    for block in range(z_size):
        for k in range(1, x_size):
            across_copy(block, lax.rem(x + k, x_size)).wait_send()


def body(
    dom_shape,
    work_shape,
    entity,
    row_state,
    relation_table,
    edge_heads,
    edge_relations,
    edge_tails,
    plan,
    negative_start,
):
    rows, features = entity.shape
    edges = edge_heads.shape[0]
    chips, cores = dom_shape
    z_size, x_size = work_shape
    domains, workers = chips * cores, z_size * x_size
    vmem = pl.BlockSpec(memory_space=pltpu.VMEM)
    smem = pl.BlockSpec(memory_space=pltpu.SMEM)
    coded = (features + 16, rows)
    counts = (
        [chips, chips, domains, domains]
        + [z_size, z_size, workers, workers]
        + [chips, chips, domains, domains]
        + [workers, workers, z_size, z_size]
    )
    entity_new, state_new = pl.pallas_call(
        functools.partial(kernel, dom_shape, work_shape),
        out_shape=(
            jax.ShapeDtypeStruct((features, rows), F32),
            jax.ShapeDtypeStruct((1, rows), F32),
        ),
        in_specs=[vmem, vmem, pl.BlockSpec(memory_space=pl.ANY), vmem, vmem, vmem, smem, smem],
        out_specs=(vmem, vmem),
        scratch_shapes=[
            pltpu.VMEM(relation_table.shape[::-1], BF16),
            pltpu.VMEM((domains, features, rows), BF16),
            pltpu.VMEM((workers, features, rows), BF16),
            pltpu.VMEM((workers,) + coded, CODE),
            pltpu.VMEM((z_size, features, rows), F32),
            pltpu.VMEM((workers,) + coded, CODE),
            pltpu.VMEM((z_size,) + coded, CODE),
            pltpu.VMEM((z_size,) + coded, CODE),
            pltpu.VMEM((domains,) + coded, CODE),
            pltpu.VMEM((features, edges), F32),
            pltpu.VMEM((features, edges), F32),
            pltpu.VMEM((features, edges), BF16),
            pltpu.VMEM((edges, features), BF16),
            pltpu.VMEM((features, edges), BF16),
            pltpu.VMEM((features, edges), BF16),
            pltpu.SemaphoreType.DMA,
        ]
        + [pltpu.SemaphoreType.DMA((count,)) for count in counts],
        compiler_params=pltpu.CompilerParams(
            collective_id=0, has_side_effects=True, vmem_limit_bytes=50 << 20
        ),
    )(
        entity.T,
        row_state.reshape(1, rows),
        relation_table.T,
        edge_heads.reshape(1, edges),
        edge_relations.reshape(1, edges),
        edge_tails.reshape(1, edges),
        plan,
        negative_start,
    )
    return entity_new.T, state_new.reshape(rows)


def axis_shapes(mesh):
    domains, workers = mesh.shape["dom"], mesh.shape["work"]
    cores = 2 if domains % 2 == 0 else 1
    x_size = max(math.isqrt(workers // 2), 1)
    while workers % x_size:
        x_size -= 1
    return (domains // cores, cores), (workers // x_size, x_size)


def solution(mesh):
    return jax.shard_map(
        functools.partial(body, *axis_shapes(mesh)),
        mesh=mesh,
        in_specs=(
            P(("dom", "work"), None),
            P(("dom", "work")),
            P(),
            P(("dom", "work")),
            P(("dom", "work")),
            P(("dom", "work")),
            P(),
            P(),
        ),
        out_specs=(P(("dom", "work"), None), P(("dom", "work"))),
        check_vma=False,
    )
```

time: 88.5 us -> 56.7 us (0.64)
  the two profiles are of different devices: /device:TPU:27 before, /device:TPU:1 now
where the time goes in v2:
time: 56.7 us; the launch traced here: 56.5 us
  Pallas kernels  47.8 us (84%)
  local copies, waits for them, and re-layouts  8.05 us (14%)
  between operations  0.66 us (1%)
    pallas_call x1, Pallas kernels, body(): pl.pallas_call(functools.partial(kernel, dom_shape, work_shape), out_shap...  47.8 us
    unnamed x18, local copies, waits for them, and re-layouts  8.05 us

profile of v2, /device:TPU:1, one launch (start us, length us, event | category | flops | bytes accessed | tf_op | source)
XLA Modules:
  0.0 56.5 jit_solution(3122209834824577423)
XLA Ops:
  0.6 0.0 copy-start
  0.6 1.9 %copy-done = bf16[4096,400]{0,1:T(8,128)(2,1)S(1)} copy-done((bf16[4096,400]{0,1:T(8,128)(2,1)S(1)}, bf16[4096,400]{0,1:T(8,128)(2,1)}, u32[]{:S(2)}) %copy-start) | copy-done | bytes 3276824
  2.6 0.0 copy-start.1
  2.6 0.9 %copy-done.1 = f32[128,400]{0,1:T(8,128)S(1)} copy-done((f32[128,400]{0,1:T(8,128)S(1)}, f32[128,400]{0,1:T(8,128)}, u32[]{:S(2)}) %copy-start.1) | copy-done | bytes 204824
  3.5 0.0 copy-start.2
  3.5 0.7 %copy-done.2 = s32[512]{0:T(512)S(1)} copy-done((s32[512]{0:T(512)S(1)}, s32[512]{0:T(512)}, u32[]{:S(2)}) %copy-start.2) | copy-done | bytes 2072
  4.2 0.0 copy-start.3
  4.2 0.7 %copy-done.3 = s32[512]{0:T(512)S(1)} copy-done((s32[512]{0:T(512)S(1)}, s32[512]{0:T(512)}, u32[]{:S(2)}) %copy-start.3) | copy-done | bytes 2072
  4.9 0.0 copy-start.4
  4.9 0.7 %copy-done.4 = s32[512]{0:T(512)S(1)} copy-done((s32[512]{0:T(512)S(1)}, s32[512]{0:T(512)}, u32[]{:S(2)}) %copy-start.4) | copy-done | bytes 2072
  5.5 0.0 copy-start.5
  5.5 0.7 %copy-done.5 = f32[128]{0:T(128)S(1)} copy-done((f32[128]{0:T(128)S(1)}, f32[128]{0:T(128)}, u32[]{:S(2)}) %copy-start.5) | copy-done | bytes 536
  6.2 0.0 copy-start.6
  6.2 0.7 %copy-done.6 = s32[4]{0:T(128)S(1)} copy-done((s32[4]{0:T(128)S(1)}, s32[4]{0:T(128)}, u32[]{:S(2)}) %copy-start.6) | copy-done | bytes 40
  6.8 0.0 copy-start.7
  6.9 0.7 %copy-done.7 = s32[4]{0:T(128)S(1)} copy-done((s32[4]{0:T(128)S(1)}, s32[4]{0:T(128)}, u32[]{:S(2)}) %copy-start.7) | copy-done | bytes 40
  7.5 47.8 %shard_map.95 = (f32[400,128]{1,0:T(8,128)S(1)}, f32[1,128]{1,0:T(1,128)S(1)}) custom-call(f32[400,128]{1,0:T(8,128)S(1)} %bitcast.9, f32[1,128]{1,0:T(1,128)S(1)} %bitcast.14, bf16[400,4096]{1,0:T(8,128)(2,1)S(1)} %bitcast.8, s32[1,512]{1,0:T(1,128)S(1)} %bitcast.11, s32[1,512]{1,0:T(1,128)S(1)} %bitcast.12, s32[1,512]{1,0:T(1,128)S(1)} %bitcast.13, ...), custom_call_target="tpu_custom_call" | custom-call | tf_op jit(solution)/shard_map/pallas_call | solution.py:390
  55.3 0.7 %copy.12 = f32[128,400]{0,1:T(8,128)} copy(f32[128,400]{0,1:T(8,128)S(1)} %bitcast.10) | data formatting | bytes 409600
  56.0 0.5 copy.13
Async XLA Ops:
  0.6 1.9 %copy-start = (bf16[4096,400]{0,1:T(8,128)(2,1)S(1)}, bf16[4096,400]{0,1:T(8,128)(2,1)}, u32[]{:S(2)}) copy-start(bf16[4096,400]{0,1:T(8,128)(2,1)} %param.10) | copy-start | bytes 9830404
  2.6 0.9 %copy-start.1 = (f32[128,400]{0,1:T(8,128)S(1)}, f32[128,400]{0,1:T(8,128)}, u32[]{:S(2)}) copy-start(f32[128,400]{0,1:T(8,128)} %param.8) | copy-start | bytes 614404
  3.5 0.7 %copy-start.2 = (s32[512]{0:T(512)S(1)}, s32[512]{0:T(512)}, u32[]{:S(2)}) copy-start(s32[512]{0:T(512)} %param.11) | copy-start | bytes 6148
  4.2 0.7 %copy-start.3 = (s32[512]{0:T(512)S(1)}, s32[512]{0:T(512)}, u32[]{:S(2)}) copy-start(s32[512]{0:T(512)} %param.12) | copy-start | bytes 6148
  4.9 0.7 %copy-start.4 = (s32[512]{0:T(512)S(1)}, s32[512]{0:T(512)}, u32[]{:S(2)}) copy-start(s32[512]{0:T(512)} %param.13) | copy-start | bytes 6148
  5.5 0.7 %copy-start.5 = (f32[128]{0:T(128)S(1)}, f32[128]{0:T(128)}, u32[]{:S(2)}) copy-start(f32[128]{0:T(128)} %param.9) | copy-start | bytes 1540
  6.2 0.7 %copy-start.6 = (s32[4]{0:T(128)S(1)}, s32[4]{0:T(128)}, u32[]{:S(2)}) copy-start(s32[4]{0:T(128)} %plan_ref.1) | copy-start | bytes 52
  6.8 0.7 %copy-start.7 = (s32[4]{0:T(128)S(1)}, s32[4]{0:T(128)}, u32[]{:S(2)}) copy-start(s32[4]{0:T(128)} %start_ref.1) | copy-start | bytes 52

commit v3 on v2

--- a/solution.py
+++ b/solution.py
@@ -123,37 +123,46 @@
 def kernel(
     dom_shape,
     work_shape,
+    entity_hbm,
+    state_hbm,
+    relation_hbm,
+    heads_hbm,
+    relations_hbm,
+    tails_hbm,
+    plan_hbm,
+    start_hbm,
+    entity_out,
+    state_out,
     entity_ref,
     state_ref,
-    relation_hbm,
+    relation_vmem,
     heads_ref,
     relations_ref,
     tails_ref,
     plan_ref,
     start_ref,
-    entity_out,
-    state_out,
-    relation_vmem,
     parts,
     target_part,
     partial,
     own_partial,
+    negative,
     across,
     along_out,
     along_in,
     returned,
     rel_t,
+    tail_rows,
     pulled,
     query_t,
     query_e,
     tail_hi,
     tail_lo,
-    relation_sem,
+    load_sem,
     *sems,
 ):
-    features, rows = entity_ref.shape
+    features, rows = entity_hbm.shape
     half = features // 2
-    edges = heads_ref.shape[1]
+    edges = heads_hbm.shape[1]
     relations = relation_hbm.shape[1]
     chips, cores = dom_shape
     z_size, x_size = work_shape
@@ -163,8 +172,21 @@
     y, core = dom // cores, lax.rem(dom, cores)
     z, x = me // x_size, lax.rem(me, x_size)
 
-    relation_copy = pltpu.make_async_copy(relation_hbm, relation_vmem, relation_sem)
-    relation_copy.start()
+    pairs = (
+        (entity_hbm, entity_ref),
+        (heads_hbm, heads_ref),
+        (relations_hbm, relations_ref),
+        (tails_hbm, tails_ref),
+        (plan_hbm, plan_ref),
+        (start_hbm, start_ref),
+        (state_hbm, state_ref),
+        (relation_hbm, relation_vmem),
+    )
+    loads = [
+        pltpu.make_async_copy(source, to, load_sem.at[i]) for i, (source, to) in enumerate(pairs)
+    ]
+    for load in loads:
+        load.start()
 
     def dom_device(index):
         return (index, me)
@@ -188,24 +210,20 @@
                 barrier, inc=1, device_id=exchange.peer(0, k), device_id_type=MESH
             )
 
+    loads[0].wait()
     table_t = entity_ref[...].astype(BF16)
     parts[dom] = table_t
     pl.semaphore_wait(barrier, chips + cores + z_size + x_size - 4)
     part_exchange.start()
 
+    for load in loads[1:]:
+        load.wait()
     head_local = heads_ref[...] - me * rows
     head_hot = (
         lax.broadcasted_iota(jnp.int32, (rows, edges), 0) == head_local
     ).astype(F32).astype(BF16)
     head_t = dot_nn(table_t, head_hot)
 
-    for k in range(1, chips):
-        part_exchange.forward(k)
-    part_exchange.collect()
-    target_part[me] = parts[plan_ref[dom]]
-    target_exchange.start()
-
-    relation_copy.wait()
     rel_t[...] = jnp.zeros_like(rel_t)
     step_rows = 256
 
@@ -217,10 +235,13 @@
         return carry
 
     steps = relations // step_rows
-    for k in range(1, z_size + 1):
-        lax.fori_loop((k - 1) * steps // z_size, k * steps // z_size, relation_step, 0)
-        if k < z_size:
-            target_exchange.forward(k)
+    for k in range(1, chips + 1):
+        lax.fori_loop((k - 1) * steps // chips, k * steps // chips, relation_step, 0)
+        if k < chips:
+            part_exchange.forward(k)
+    part_exchange.collect()
+    target_part[me] = parts[plan_ref[dom]]
+    target_exchange.start()
 
     rel_x, rel_y = rel_t[:half], rel_t[half:]
     head_x, head_y = head_t[:half], head_t[half:]
@@ -232,33 +253,48 @@
     query_float = query_bf.astype(F32)
     query_e[...] = untranspose_pad(query_float).astype(BF16)
 
-    target_exchange.collect()
-
     width = x_size * rows
+    factor = 1.0 / math.sqrt(NEG)
+    first_negative = start_ref[dom]
 
     def tail_hot(block):
         row = lax.broadcasted_iota(jnp.int32, (width, edges), 0) + block * width
         return (row == tails_ref[...]).astype(F32).astype(BF16)
 
-    def block_of(block):
-        return jnp.concatenate([target_part[block * x_size + j] for j in range(x_size)], axis=1)
-
+    tail_rows[...] = jnp.zeros_like(tail_rows)
     pulled[...] = jnp.zeros_like(pulled)
 
-    def tail_step(block, carry):
-        pulled[...] += dot_nn(block_of(block), tail_hot(block))
+    def score_step(k, carry):
+        @pl.when(k < z_size - 1)
+        def _():
+            target_exchange.forward(k + 1)
+
+        for kb in range(1, x_size):
+            target_exchange.second(k, kb, True).wait_recv()
+        block = lax.rem(z + z_size - k, z_size)
+        part = jnp.concatenate(
+            [target_part[block * x_size + j] for j in range(x_size)], axis=1
+        )
+        tail_rows[...] += dot_nn(part, tail_hot(block))
+        scores = dot_nn(query_e[...], part)
+        weights = jax.nn.sigmoid(scores) * factor
+        if part_rows > NEG:
+            row = lax.broadcasted_iota(jnp.int32, (1, width), 1) + block * width
+            offset = row - first_negative
+            offset = jnp.where(offset < 0, offset + part_rows, offset)
+            weights = jnp.where(offset < NEG, weights, 0.0)
+        weights = weights.astype(BF16)
+        pulled[...] += dot_nt(part, weights)
+        negative[block] = dot_nn(query_t[...], weights)
         return carry
 
-    lax.fori_loop(0, z_size, tail_step, 0)
-    tail_t = pulled[...]
+    lax.fori_loop(0, z_size, score_step, 0)
+    tail_t = tail_rows[...]
     positive = jnp.sum(query_float * tail_t, axis=0, keepdims=True)
     positive_weight = jax.nn.sigmoid(positive) - 1.0
-    pulled[...] = positive_weight * tail_t
     high, low = split(positive_weight * query_float)
     tail_hi[...] = high
     tail_lo[...] = low
-    factor = 1.0 / math.sqrt(NEG)
-    first_negative = start_ref[dom]
 
     def across_copy(block, j, arriving=False):
         k = lax.rem(j - x + x_size, x_size)
@@ -282,21 +318,10 @@
             device_id_type=MESH,
         )
 
-    def score_step(step, carry):
+    def send_step(step, carry):
         block = lax.rem(z + step + 1, z_size)
-        part = block_of(block)
-        scores = dot_nn(query_e[...], part)
-        weights = jax.nn.sigmoid(scores) * factor
-        if part_rows > NEG:
-            row = lax.broadcasted_iota(jnp.int32, (1, width), 1) + block * width
-            offset = row - first_negative
-            offset = jnp.where(offset < 0, offset + part_rows, offset)
-            weights = jnp.where(offset < NEG, weights, 0.0)
-        weights = weights.astype(BF16)
         hot = tail_hot(block)
-        grad = (
-            dot_nn(query_t[...], weights) + dot_nt(tail_hi[...], hot) + dot_nt(tail_lo[...], hot)
-        )
+        grad = negative[block] + dot_nt(tail_hi[...], hot) + dot_nt(tail_lo[...], hot)
         for j in range(x_size):
             piece = grad[:, j * rows : (j + 1) * rows]
 
@@ -309,13 +334,13 @@
                 store_code(partial, block * x_size + j, piece)
                 across_copy(block, j).start()
 
-        pulled[...] += dot_nt(part, weights)
         return carry
 
-    lax.fori_loop(0, z_size, score_step, 0)
+    lax.fori_loop(0, z_size, send_step, 0)
 
     def own_gradient():
-        grad_x, grad_y = pulled[:half], pulled[half:]
+        grad_t = positive_weight * tail_rows[...] + pulled[...]
+        grad_x, grad_y = grad_t[:half], grad_t[half:]
         rel_x, rel_y = rel_t[:half], rel_t[half:]
         head_grad = jnp.concatenate(
             [grad_x * rel_x + grad_y * rel_y, grad_y * rel_x - grad_x * rel_y], axis=0
@@ -379,7 +404,6 @@
     z_size, x_size = work_shape
     domains, workers = chips * cores, z_size * x_size
     vmem = pl.BlockSpec(memory_space=pltpu.VMEM)
-    smem = pl.BlockSpec(memory_space=pltpu.SMEM)
     coded = (features + 16, rows)
     counts = (
         [chips, chips, domains, domains]
@@ -393,29 +417,38 @@
             jax.ShapeDtypeStruct((features, rows), F32),
             jax.ShapeDtypeStruct((1, rows), F32),
         ),
-        in_specs=[vmem, vmem, pl.BlockSpec(memory_space=pl.ANY), vmem, vmem, vmem, smem, smem],
+        in_specs=[pl.BlockSpec(memory_space=pltpu.HBM)] * 8,
         out_specs=(vmem, vmem),
         scratch_shapes=[
+            pltpu.VMEM((features, rows), F32),
+            pltpu.VMEM((1, rows), F32),
             pltpu.VMEM(relation_table.shape[::-1], BF16),
+            pltpu.VMEM((1, edges), jnp.int32),
+            pltpu.VMEM((1, edges), jnp.int32),
+            pltpu.VMEM((1, edges), jnp.int32),
+            pltpu.SMEM(plan.shape, jnp.int32),
+            pltpu.SMEM(negative_start.shape, jnp.int32),
             pltpu.VMEM((domains, features, rows), BF16),
             pltpu.VMEM((workers, features, rows), BF16),
             pltpu.VMEM((workers,) + coded, CODE),
             pltpu.VMEM((z_size, features, rows), F32),
+            pltpu.VMEM((z_size, features, x_size * rows), F32),
             pltpu.VMEM((workers,) + coded, CODE),
             pltpu.VMEM((z_size,) + coded, CODE),
             pltpu.VMEM((z_size,) + coded, CODE),
             pltpu.VMEM((domains,) + coded, CODE),
             pltpu.VMEM((features, edges), F32),
             pltpu.VMEM((features, edges), F32),
+            pltpu.VMEM((features, edges), F32),
             pltpu.VMEM((features, edges), BF16),
             pltpu.VMEM((edges, features), BF16),
             pltpu.VMEM((features, edges), BF16),
             pltpu.VMEM((features, edges), BF16),
-            pltpu.SemaphoreType.DMA,
+            pltpu.SemaphoreType.DMA((8,)),
         ]
         + [pltpu.SemaphoreType.DMA((count,)) for count in counts],
         compiler_params=pltpu.CompilerParams(
-            collective_id=0, has_side_effects=True, vmem_limit_bytes=50 << 20
+            collective_id=0, has_side_effects=True, vmem_limit_bytes=56 << 20
         ),
     )(
         entity.T,

time: 56.7 us -> 49.6 us (0.87)
  local copies, waits for them, and re-layouts: 8.05 us -> 2.74 us
  Pallas kernels: 47.8 us -> 46.1 us
    unnamed x18 -> x2, local copies, waits for them, and re-layouts: 8.05 us -> 2.74 us
    pallas_call x1, Pallas kernels: 47.8 us -> 46.1 us  [body(): pl.pallas_call(functools.partial(kernel, dom_shape, work_shape), out_shap...]
where the time goes in v3:
time: 49.6 us; the launch traced here: 49.4 us
  Pallas kernels  46.1 us (93%)
  local copies, waits for them, and re-layouts  2.74 us (6%)
  between operations  0.64 us (1%)
    pallas_call x1, Pallas kernels, body(): pl.pallas_call(functools.partial(kernel, dom_shape, work_shape), out_shap...  46.1 us
    unnamed x2, local copies, waits for them, and re-layouts  2.74 us

profile of v3, /device:TPU:1, one launch (start us, length us, event | category | flops | bytes accessed | tf_op | source)
XLA Modules:
  0.0 49.4 jit_solution(14897825947555556127)
XLA Ops:
  0.6 46.1 %shard_map.95 = (f32[400,128]{1,0:T(8,128)}, f32[1,128]{1,0:T(1,128)}) custom-call(f32[400,128]{1,0:T(8,128)} %bitcast.9, f32[1,128]{1,0:T(1,128)} %bitcast.14, bf16[400,4096]{1,0:T(8,128)(2,1)} %bitcast.8, s32[1,512]{1,0:T(1,128)} %bitcast.11, s32[1,512]{1,0:T(1,128)} %bitcast.12, s32[1,512]{1,0:T(1,128)} %bitcast.13, s32[4]{0:T(128)} %plan_hbm.1, s32[4]{0:T(128)} %start_hbm.1), custom_call_target="tpu_custom_call" | custom-call | tf_op jit(solution)/shard_map/pallas_call | solution.py:414
  46.7 1.6 %copy.12 = f32[128,400]{0,1:T(8,128)} copy(f32[128,400]{0,1:T(8,128)} %bitcast.10) | data formatting | bytes 409600
  48.3 1.1 %copy.13 = f32[128]{0:T(128)} copy(f32[128]{0:T(128)} %bitcast.15) | data formatting | bytes 1024

commit v4 on v3

--- a/solution.py
+++ b/solution.py
@@ -225,7 +225,7 @@
     head_t = dot_nn(table_t, head_hot)
 
     rel_t[...] = jnp.zeros_like(rel_t)
-    step_rows = 256
+    step_rows = 512
 
     def relation_step(step, carry):
         base = pl.multiple_of(step * step_rows, step_rows)
@@ -358,7 +358,7 @@
         if step < z_size:
             store_code(along_out, step, total)
             along_copy(step).start()
-        if step == 1:
+        if step == z_size - 1:
             own_grad = own_gradient()
     for k in range(1, z_size):
         along_copy(k).wait_recv()

time: 49.6 us -> 48.6 us (0.980)
  Pallas kernels: 46.1 us -> 45.1 us
    pallas_call x1, Pallas kernels: 46.1 us -> 45.1 us  [body(): pl.pallas_call(functools.partial(kernel, dom_shape, work_shape), out_shap...]
where the time goes in v4:
time: 48.6 us; the launch traced here: 48.4 us
  Pallas kernels  45.1 us (93%)
  local copies, waits for them, and re-layouts  2.74 us (6%)
  between operations  0.64 us (1%)
    pallas_call x1, Pallas kernels, body(): pl.pallas_call(functools.partial(kernel, dom_shape, work_shape), out_shap...  45.1 us
    unnamed x2, local copies, waits for them, and re-layouts  2.74 us

profile of v4, /device:TPU:1, one launch (start us, length us, event | category | flops | bytes accessed | tf_op | source)
XLA Modules:
  0.0 48.4 jit_solution(5255661946399926510)
XLA Ops:
  0.6 45.1 %shard_map.95 = (f32[400,128]{1,0:T(8,128)}, f32[1,128]{1,0:T(1,128)}) custom-call(f32[400,128]{1,0:T(8,128)} %bitcast.9, f32[1,128]{1,0:T(1,128)} %bitcast.14, bf16[400,4096]{1,0:T(8,128)(2,1)} %bitcast.8, s32[1,512]{1,0:T(1,128)} %bitcast.11, s32[1,512]{1,0:T(1,128)} %bitcast.12, s32[1,512]{1,0:T(1,128)} %bitcast.13, s32[4]{0:T(128)} %plan_hbm.1, s32[4]{0:T(128)} %start_hbm.1), custom_call_target="tpu_custom_call" | custom-call | tf_op jit(solution)/shard_map/pallas_call | solution.py:414
  45.7 1.6 %copy.12 = f32[128,400]{0,1:T(8,128)} copy(f32[128,400]{0,1:T(8,128)} %bitcast.10) | data formatting | bytes 409600
  47.3 1.1 %copy.13 = f32[128]{0:T(128)} copy(f32[128]{0:T(128)} %bitcast.15) | data formatting | bytes 1024

commit v5 on v4

--- a/solution.py
+++ b/solution.py
@@ -199,6 +199,65 @@
     return_exchange = Exchange(returned, dom_device, y, core, chips, cores, sems[8:12])
     across_send, across_recv, along_send, along_recv = sems[12:16]
 
+    def hop(source, way):
+        slot = source * x_size + x
+        return pltpu.make_async_remote_copy(
+            src_ref=target_part.at[slot],
+            dst_ref=target_part.at[slot],
+            send_sem=sems[4].at[source + (z_size if way < 0 else 0)],
+            recv_sem=sems[5].at[source],
+            device_id=(dom, jnp.clip(z + way, 0, z_size - 1) * x_size + x),
+            device_id_type=MESH,
+        )
+
+    def side(source, kb, arriving=False):
+        slot = source * x_size + (lax.rem(x + x_size - kb, x_size) if arriving else x)
+        at = source * x_size + kb
+        return pltpu.make_async_remote_copy(
+            src_ref=target_part.at[slot],
+            dst_ref=target_part.at[slot],
+            send_sem=sems[6].at[at],
+            recv_sem=sems[7].at[at],
+            device_id=(dom, z * x_size + lax.rem(x + kb, x_size)),
+            device_id_type=MESH,
+        )
+
+    def chain_start():
+        @pl.when(z < z_size - 1)
+        def _():
+            hop(z, 1).start()
+
+        @pl.when(z > 0)
+        def _():
+            hop(z, -1).start()
+
+        for kb in range(1, x_size):
+            side(z, kb).start()
+
+    def chain_forward(source, way):
+        hop(source, way).wait_recv()
+
+        @pl.when((z + way >= 0) & (z + way < z_size))
+        def _():
+            hop(source, way).start()
+
+        for kb in range(1, x_size):
+            side(source, kb).start()
+
+    def chain_finish():
+        for source in range(z_size):
+
+            @pl.when((z >= source) & (z < z_size - 1))
+            def _():
+                hop(source, 1).wait_send()
+
+            @pl.when((z <= source) & (z > 0))
+            def _():
+                hop(source, -1).wait_send()
+
+            for kb in range(1, x_size):
+                side(source, kb).wait_send()
+
     barrier = pltpu.get_barrier_semaphore()
     for exchange in (part_exchange, target_exchange):
         for k in range(1, exchange.a_size):
@@ -241,7 +300,7 @@
             part_exchange.forward(k)
     part_exchange.collect()
     target_part[me] = parts[plan_ref[dom]]
-    target_exchange.start()
+    chain_start()
 
     rel_x, rel_y = rel_t[:half], rel_t[half:]
     head_x, head_y = head_t[:half], head_t[half:]
@@ -264,14 +323,18 @@
     tail_rows[...] = jnp.zeros_like(tail_rows)
     pulled[...] = jnp.zeros_like(pulled)
 
-    def score_step(k, carry):
-        @pl.when(k < z_size - 1)
-        def _():
-            target_exchange.forward(k + 1)
-
+    def arrivals(distance):
+        @pl.when(z - distance >= 0)
+        def _():
+            chain_forward(z - distance, 1)
+
+        @pl.when(z + distance < z_size)
+        def _():
+            chain_forward(z + distance, -1)
+
+    def score_block(block):
         for kb in range(1, x_size):
-            target_exchange.second(k, kb, True).wait_recv()
-        block = lax.rem(z + z_size - k, z_size)
+            side(block, kb, True).wait_recv()
         part = jnp.concatenate(
             [target_part[block * x_size + j] for j in range(x_size)], axis=1
         )
@@ -286,6 +349,20 @@
         weights = weights.astype(BF16)
         pulled[...] += dot_nt(part, weights)
         negative[block] = dot_nn(query_t[...], weights)
+
+    def score_step(distance, carry):
+        @pl.when(distance < z_size - 1)
+        def _():
+            arrivals(distance + 1)
+
+        @pl.when(z - distance >= 0)
+        def _():
+            score_block(z - distance)
+
+        @pl.when((distance > 0) & (z + distance < z_size))
+        def _():
+            score_block(z + distance)
+
         return carry
 
     lax.fori_loop(0, z_size, score_step, 0)
@@ -377,7 +454,7 @@
     entity_out[...] = entity_ref[...] - learn_rate * gradient / jnp.sqrt(state_new)
 
     part_exchange.finish()
-    target_exchange.finish()
+    chain_finish()
     return_exchange.finish()
     for k in range(1, z_size):
         along_copy(k).wait_send()
@@ -407,7 +484,7 @@
     coded = (features + 16, rows)
     counts = (
         [chips, chips, domains, domains]
-        + [z_size, z_size, workers, workers]
+        + [2 * z_size, z_size, workers, workers]
         + [chips, chips, domains, domains]
         + [workers, workers, z_size, z_size]
     )

time: 48.6 us -> 46.9 us (0.965)
  Pallas kernels: 45.1 us -> 43.4 us
    pallas_call x1, Pallas kernels: 45.1 us -> 43.4 us  [body(): pl.pallas_call(functools.partial(kernel, dom_shape, work_shape), out_shap...]
where the time goes in v5:
time: 46.9 us; the launch traced here: 46.8 us
  Pallas kernels  43.4 us (93%)
  local copies, waits for them, and re-layouts  2.74 us (6%)
  between operations  0.64 us (1%)
    pallas_call x1, Pallas kernels, body(): pl.pallas_call(functools.partial(kernel, dom_shape, work_shape), out_shap...  43.4 us
    unnamed x2, local copies, waits for them, and re-layouts  2.74 us

profile of v5, /device:TPU:1, one launch (start us, length us, event | category | flops | bytes accessed | tf_op | source)
XLA Modules:
  0.0 46.8 jit_solution(1514004424885349162)
XLA Ops:
  0.6 43.4 %shard_map.95 = (f32[400,128]{1,0:T(8,128)}, f32[1,128]{1,0:T(1,128)}) custom-call(f32[400,128]{1,0:T(8,128)} %bitcast.9, f32[1,128]{1,0:T(1,128)} %bitcast.14, bf16[400,4096]{1,0:T(8,128)(2,1)} %bitcast.8, s32[1,512]{1,0:T(1,128)} %bitcast.11, s32[1,512]{1,0:T(1,128)} %bitcast.12, s32[1,512]{1,0:T(1,128)} %bitcast.13, s32[4]{0:T(128)} %plan_hbm.1, s32[4]{0:T(128)} %start_hbm.1), custom_call_target="tpu_custom_call" | custom-call | tf_op jit(solution)/shard_map/pallas_call | solution.py:491
  44.0 1.6 %copy.12 = f32[128,400]{0,1:T(8,128)} copy(f32[128,400]{0,1:T(8,128)} %bitcast.10) | data formatting | bytes 409600
  45.7 1.1 %copy.13 = f32[128]{0:T(128)} copy(f32[128]{0:T(128)} %bitcast.15) | data formatting | bytes 1024
